TPU v7x, 32 devices: a whole 2x2x4 slice. The times are simulated.
32 devices in a mesh: dp: 4 (over y, x), ctx: 2 (over core), tensor: 4 (over z).
Axes of the slice: x: 2, y: 2, z: 4, core: 2. Of those that a mesh axis runs over, the one named last changes fastest.
Arguments:
- inputs: bfloat16 [4, 1024, 2048], P('dp', 'ctx'), may hold values from -6 to 6
- segment_ids: int32 [4, 1024], P('dp', 'ctx'), may hold values from -1 to 1022, as said below
- attention_gain: float32 [2048], replicated, may hold values from 0.5 to 1.5
- query_weight: bfloat16 [2048, 2048], P(None, 'tensor'), may hold values from -0.125 to 0.125
- key_weight: bfloat16 [2048, 256], P(None, 'tensor'), may hold values from -0.125 to 0.125
- value_weight: bfloat16 [2048, 256], P(None, 'tensor'), may hold values from -0.125 to 0.125
- out_weight: bfloat16 [2048, 2048], P('tensor'), may hold values from -0.75 to 0.75
- feedforward_gain: float32 [2048], replicated, may hold values from 0.5 to 1.5
- gate_weight: bfloat16 [2048, 5632], P(None, 'tensor'), may hold values from -0.125 to 0.125
- up_weight: bfloat16 [2048, 5632], P(None, 'tensor'), may hold values from -0.125 to 0.125
- down_weight: bfloat16 [5632, 2048], P('tensor'), may hold values from -0.078125 to 0.078125
- cotangent: bfloat16 [4, 1024, 2048], P('dp', 'ctx'), may hold values from -6 to 6
Outputs:
- layer_out: bfloat16 [4, 1024, 2048], P('dp', 'ctx')
- grad_inputs: bfloat16 [4, 1024, 2048], P('dp', 'ctx')
- grad_attention_gain: float32 [2048], P(('dp', 'ctx'))
- grad_query_weight: float32 [2048, 2048], P(('dp', 'ctx'), 'tensor')
- grad_key_weight: float32 [2048, 256], P(('dp', 'ctx'), 'tensor')
- grad_value_weight: float32 [2048, 256], P(('dp', 'ctx'), 'tensor')
- grad_out_weight: float32 [2048, 2048], P('tensor', ('dp', 'ctx'))
- grad_feedforward_gain: float32 [2048], P(('dp', 'ctx'))
- grad_gate_weight: float32 [2048, 5632], P(('dp', 'ctx'), 'tensor')
- grad_up_weight: float32 [2048, 5632], P(('dp', 'ctx'), 'tensor')
- grad_down_weight: float32 [5632, 2048], P('tensor', ('dp', 'ctx'))
Inputs may be any that keep to these rules, and one draw needn't show every extreme that they name: `segment_ids`: along each sequence the numbers start at 0 and rise by at most one from token to token over the documents; the last 1 to 128 tokens of every sequence are padding, marked -1. In every draw the first sequence holds documents of one token each and a single padding token.
All inputs are finite; a program needn't handle non-finite values.
Results may differ from a plain program's by a relative error of at most 0.018.
Values may be sent and summed in bfloat16 or wider, within the bound.
A program may use at most 192 MiB of HBM per device.

v0:
```python
import math

import jax
import jax.numpy as jnp
from jax import lax
from jax.sharding import PartitionSpec as P

HEAD_DIM = 64


epsilon = 1e-05
rope_base = 10000.0
masked_score = -1e30


def positions_of(segment):
    token_index = jnp.arange(segment.shape[-1], dtype=jnp.int32)
    previous = jnp.concatenate([segment[..., :1] - 1, segment[..., :-1]], axis=-1)
    starts = jnp.where(segment != previous, token_index, 0)
    return token_index - lax.cummax(starts, axis=segment.ndim - 1)


def rotary_tables(positions):
    half_dim = HEAD_DIM // 2
    frequency = rope_base ** (-2.0 * jnp.arange(half_dim, dtype=jnp.float32) / HEAD_DIM)
    angles = positions.astype(jnp.float32)[..., None] * frequency
    return (jnp.cos(angles), jnp.sin(angles))


def rotate(values, cosine, sine_table):
    half_dim = values.shape[-1] // 2
    first = values[..., :half_dim]
    second = values[..., half_dim:]
    return jnp.concatenate(
        [first * cosine - second * sine_table, second * cosine + first * sine_table], axis=-1
    )


def visible(query_seg, key_seg, first_row):
    query_pos = first_row + jnp.arange(query_seg.shape[0], dtype=jnp.int32)
    key_pos = jnp.arange(key_seg.shape[0], dtype=jnp.int32)
    same_doc = query_seg[:, None] == key_seg[None, :]
    causal = key_pos[None, :] <= query_pos[:, None]
    usable = (key_seg[None, :] >= 0) | (key_pos[None, :] == query_pos[:, None])
    return same_doc & causal & usable


def body(
    inputs,
    segment_ids,
    attention_gain,
    query_weight,
    key_weight,
    value_weight,
    out_weight,
    feedforward_gain,
    gate_weight,
    up_weight,
    down_weight,
    cotangent,
):
    seq_count, span_len, model_width = inputs.shape
    row_count = seq_count * span_len
    query_heads = query_weight.shape[1] // HEAD_DIM
    kv_heads = key_weight.shape[1] // HEAD_DIM
    group_size = query_heads // kv_heads
    score_scale = 1.0 / math.sqrt(HEAD_DIM)
    offset = lax.axis_index("ctx") * span_len
    whole_segments = lax.all_gather(segment_ids, "ctx", axis=1, tiled=True)
    own_positions = lax.dynamic_slice_in_dim(positions_of(whole_segments), offset, span_len, 1)
    cosine, sine_table = rotary_tables(own_positions)
    cosine = cosine[:, :, None, :]
    sine_table = sine_table[:, :, None, :]
    hidden = inputs.astype(jnp.float32).reshape(row_count, model_width)
    inverse_one = lax.rsqrt(jnp.mean(hidden * hidden, axis=-1, keepdims=True) + epsilon)
    unit_one = hidden * inverse_one
    normed = (unit_one * attention_gain).astype(jnp.bfloat16)
    query_rows = rotate(
        jnp.dot(normed, query_weight, preferred_element_type=jnp.float32).reshape(
            seq_count, span_len, query_heads, HEAD_DIM
        ),
        cosine,
        sine_table,
    ).astype(jnp.bfloat16)
    key_rows = rotate(
        jnp.dot(normed, key_weight, preferred_element_type=jnp.float32).reshape(
            seq_count, span_len, kv_heads, HEAD_DIM
        ),
        cosine,
        sine_table,
    ).astype(jnp.bfloat16)
    value_rows = (
        jnp.dot(normed, value_weight, preferred_element_type=jnp.float32)
        .astype(jnp.bfloat16)
        .reshape(seq_count, span_len, kv_heads, HEAD_DIM)
    )
    all_keys, all_values = (
        lax.all_gather(key_rows, "ctx", axis=1, tiled=True),
        lax.all_gather(value_rows, "ctx", axis=1, tiled=True),
    )

    def attend(block_items):
        query_block, key_block, value_block, query_seg, key_seg = block_items
        allowed = visible(query_seg, key_seg, offset)
        grouped = query_block.reshape(span_len, kv_heads, group_size, HEAD_DIM)
        raw_scores = jnp.einsum(
            "qhgd,khd->hgqk", grouped, key_block, preferred_element_type=jnp.float32
        )
        scores = jnp.where(allowed, raw_scores * score_scale, masked_score)
        row_peak = jnp.max(scores, axis=-1, keepdims=True)
        shifted_exp = jnp.exp(scores - row_peak)
        denominator = jnp.sum(shifted_exp, axis=-1, keepdims=True)
        attn_probs = (shifted_exp / denominator).astype(jnp.bfloat16)
        mixed_block = jnp.einsum(
            "hgqk,khd->qhgd", attn_probs, value_block, preferred_element_type=jnp.float32
        )
        return (
            mixed_block.astype(jnp.bfloat16).reshape(span_len, query_heads * HEAD_DIM),
            row_peak + jnp.log(denominator),
        )

    mixed_heads, log_sums = lax.map(
        attend, (query_rows, all_keys, all_values, segment_ids, whole_segments)
    )
    mixed_flat = mixed_heads.reshape(row_count, query_heads * HEAD_DIM)
    attended = lax.psum(
        jnp.dot(mixed_flat, out_weight, preferred_element_type=jnp.float32), "tensor"
    )
    middle = hidden + attended
    inverse_two = lax.rsqrt(jnp.mean(middle * middle, axis=-1, keepdims=True) + epsilon)
    unit_two = middle * inverse_two
    normed_two = (unit_two * feedforward_gain).astype(jnp.bfloat16)
    gate_pre = jnp.dot(normed_two, gate_weight, preferred_element_type=jnp.float32)
    up_pre = jnp.dot(normed_two, up_weight, preferred_element_type=jnp.float32)
    sigmoid_gate = jax.nn.sigmoid(gate_pre)
    inner_act = (gate_pre * sigmoid_gate * up_pre).astype(jnp.bfloat16)
    feed_out = lax.psum(
        jnp.dot(inner_act, down_weight, preferred_element_type=jnp.float32).astype(jnp.bfloat16),
        "tensor",
    ).astype(jnp.float32)
    layer_out = (middle + feed_out).astype(jnp.bfloat16).reshape(seq_count, span_len, model_width)
    upstream = cotangent.reshape(row_count, model_width)
    grad_down = jnp.dot(inner_act.T, upstream, preferred_element_type=jnp.float32)
    grad_inner = jnp.dot(upstream, down_weight.T, preferred_element_type=jnp.float32)
    grad_up_pre = (grad_inner * gate_pre * sigmoid_gate).astype(jnp.bfloat16)
    grad_gate_pre = (
        grad_inner * up_pre * sigmoid_gate * (1.0 + gate_pre * (1.0 - sigmoid_gate))
    ).astype(jnp.bfloat16)
    grad_gate = jnp.dot(normed_two.T, grad_gate_pre, preferred_element_type=jnp.float32)
    grad_up = jnp.dot(normed_two.T, grad_up_pre, preferred_element_type=jnp.float32)
    grad_normed_two = lax.psum(
        jnp.dot(grad_gate_pre, gate_weight.T, preferred_element_type=jnp.float32)
        + jnp.dot(grad_up_pre, up_weight.T, preferred_element_type=jnp.float32),
        "tensor",
    )
    grad_ffn_gain = jnp.sum(grad_normed_two * unit_two, axis=0)
    scaled_two = grad_normed_two * feedforward_gain
    grad_middle = upstream.astype(jnp.float32) + inverse_two * (
        scaled_two - unit_two * jnp.mean(scaled_two * unit_two, axis=-1, keepdims=True)
    )
    grad_attended = grad_middle.astype(jnp.bfloat16)
    grad_out_part = jnp.dot(mixed_flat.T, grad_attended, preferred_element_type=jnp.float32)
    grad_mixed = (
        jnp.dot(grad_attended, out_weight.T, preferred_element_type=jnp.float32)
        .astype(jnp.bfloat16)
        .reshape(seq_count, span_len, query_heads, HEAD_DIM)
    )

    def attend_back(block_items):
        query_block, key_block, value_block, query_seg, key_seg, grad_block, log_block = block_items
        allowed = visible(query_seg, key_seg, offset)
        grouped = query_block.reshape(span_len, kv_heads, group_size, HEAD_DIM)
        grad_grouped = grad_block.reshape(span_len, kv_heads, group_size, HEAD_DIM)
        raw_scores = jnp.einsum(
            "qhgd,khd->hgqk", grouped, key_block, preferred_element_type=jnp.float32
        )
        scores = jnp.where(allowed, raw_scores * score_scale, masked_score)
        attn_probs = jnp.exp(scores - log_block)
        rounded = attn_probs.astype(jnp.bfloat16)
        grad_values = jnp.einsum(
            "hgqk,qhgd->khd", rounded, grad_grouped, preferred_element_type=jnp.float32
        )
        grad_probs = jnp.einsum(
            "qhgd,khd->hgqk", grad_grouped, value_block, preferred_element_type=jnp.float32
        )
        row_dot = jnp.sum(attn_probs * grad_probs, axis=-1, keepdims=True)
        grad_scores = (attn_probs * (grad_probs - row_dot) * score_scale).astype(jnp.bfloat16)
        grad_queries = jnp.einsum(
            "hgqk,khd->qhgd", grad_scores, key_block, preferred_element_type=jnp.float32
        ).reshape(span_len, query_heads, HEAD_DIM)
        grad_keys = jnp.einsum(
            "hgqk,qhgd->khd", grad_scores, grouped, preferred_element_type=jnp.float32
        )
        return (grad_queries, grad_keys, grad_values)

    grad_queries, grad_keys, grad_values = lax.map(
        attend_back,
        (query_rows, all_keys, all_values, segment_ids, whole_segments, grad_mixed, log_sums),
    )
    own_grad_keys, own_grad_values = (
        lax.psum_scatter(grad_keys, "ctx", scatter_dimension=1, tiled=True),
        lax.psum_scatter(grad_values, "ctx", scatter_dimension=1, tiled=True),
    )
    grad_query_pre = (
        rotate(grad_queries, cosine, -sine_table)
        .astype(jnp.bfloat16)
        .reshape(row_count, query_heads * HEAD_DIM)
    )
    grad_key_pre = (
        rotate(own_grad_keys, cosine, -sine_table)
        .astype(jnp.bfloat16)
        .reshape(row_count, kv_heads * HEAD_DIM)
    )
    grad_value_pre = own_grad_values.astype(jnp.bfloat16).reshape(row_count, kv_heads * HEAD_DIM)
    grad_query = jnp.dot(normed.T, grad_query_pre, preferred_element_type=jnp.float32)
    grad_key = jnp.dot(normed.T, grad_key_pre, preferred_element_type=jnp.float32)
    grad_value = jnp.dot(normed.T, grad_value_pre, preferred_element_type=jnp.float32)
    grad_normed = lax.psum(
        (
            jnp.dot(grad_query_pre, query_weight.T, preferred_element_type=jnp.float32)
            + jnp.dot(grad_key_pre, key_weight.T, preferred_element_type=jnp.float32)
            + jnp.dot(grad_value_pre, value_weight.T, preferred_element_type=jnp.float32)
        ).astype(jnp.bfloat16),
        "tensor",
    ).astype(jnp.float32)
    grad_attn_gain = jnp.sum(grad_normed * unit_one, axis=0)
    scaled_one = grad_normed * attention_gain
    grad_hidden = grad_middle + inverse_one * (
        scaled_one - unit_one * jnp.mean(scaled_one * unit_one, axis=-1, keepdims=True)
    )
    grad_inputs = grad_hidden.astype(jnp.bfloat16).reshape(seq_count, span_len, model_width)
    reduced = (
        lax.psum_scatter(
            grad_attn_gain.astype(jnp.bfloat16), ("dp", "ctx"), scatter_dimension=0, tiled=True
        ).astype(jnp.float32),
        lax.psum_scatter(
            grad_query.astype(jnp.bfloat16), ("dp", "ctx"), scatter_dimension=0, tiled=True
        ).astype(jnp.float32),
        lax.psum_scatter(
            grad_key.astype(jnp.bfloat16), ("dp", "ctx"), scatter_dimension=0, tiled=True
        ).astype(jnp.float32),
        lax.psum_scatter(
            grad_value.astype(jnp.bfloat16), ("dp", "ctx"), scatter_dimension=0, tiled=True
        ).astype(jnp.float32),
        lax.psum_scatter(
            grad_out_part.astype(jnp.bfloat16), ("dp", "ctx"), scatter_dimension=1, tiled=True
        ).astype(jnp.float32),
        lax.psum_scatter(
            grad_ffn_gain.astype(jnp.bfloat16), ("dp", "ctx"), scatter_dimension=0, tiled=True
        ).astype(jnp.float32),
        lax.psum_scatter(
            grad_gate.astype(jnp.bfloat16), ("dp", "ctx"), scatter_dimension=0, tiled=True
        ).astype(jnp.float32),
        lax.psum_scatter(
            grad_up.astype(jnp.bfloat16), ("dp", "ctx"), scatter_dimension=0, tiled=True
        ).astype(jnp.float32),
        lax.psum_scatter(
            grad_down.astype(jnp.bfloat16), ("dp", "ctx"), scatter_dimension=1, tiled=True
        ).astype(jnp.float32),
    )
    return (
        layer_out,
        grad_inputs,
        reduced[0],
        reduced[1],
        reduced[2],
        reduced[3],
        reduced[4],
        reduced[5],
        reduced[6],
        reduced[7],
        reduced[8],
    )


def solution(mesh):
    return jax.shard_map(
        body,
        mesh=mesh,
        in_specs=(
            P("dp", "ctx", None),
            P("dp", "ctx"),
            P(),
            P(None, "tensor"),
            P(None, "tensor"),
            P(None, "tensor"),
            P("tensor", None),
            P(),
            P(None, "tensor"),
            P(None, "tensor"),
            P("tensor", None),
            P("dp", "ctx", None),
        ),
        out_specs=(
            P("dp", "ctx", None),
            P("dp", "ctx", None),
            P(("dp", "ctx")),
            P(("dp", "ctx"), "tensor"),
            P(("dp", "ctx"), "tensor"),
            P(("dp", "ctx"), "tensor"),
            P("tensor", ("dp", "ctx")),
            P(("dp", "ctx")),
            P(("dp", "ctx"), "tensor"),
            P(("dp", "ctx"), "tensor"),
            P("tensor", ("dp", "ctx")),
        ),
        check_vma=False,
    )
```

profile of v0, /device:TPU:0, one launch (start us, length us, event | category | flops | bytes accessed | tf_op | source)
XLA Modules:
  0.0 1002.4 jit_solution(10803641659905566394)
XLA Ops:
  7.3 2.2 all_gather.10
  10.0 2.1 fusion.25
  13.5 2.6 convolution_convert_fusion.9
  16.1 1.9 all-gather
  18.0 0.8 convolution_bitcast_fusion.2
  19.6 1.9 all_gather.11
  21.5 3.9 copy.33
  25.4 3.6 fusion.41
  29.2 1.0 fusion.39
  30.2 7.3 fusion.96
  37.5 8.0 fusion.4
  45.6 7.4 fusion.44
  53.0 3.3 fusion.97
  56.9 157.1 %all-reduce.8.cloned.1.call-done = f32[512,2048]{1,0:T(8,128)} async-done(((f32[512,2048]{1,0:T(8,128)}), f32[512,2048]{1,0:T(8,128)}) %all-reduce.8.cloned.1.call-update) | async-done | bytes 4194320 | tf_op jit(solution)/shard_map/psum | solution.py:126
  214.0 3.5 multiply_reduce_fusion.2
  218.0 10.1 %fusion.99 = f32[512,1408]{1,0:T(8,128)} fusion(bf16[512,2048]{1,0:T(8,128)(2,1)S(1)} %multiply_convert_fusion, bf16[2048,1408]{1,0:T(8,128)(2,1)} %param.21), kind=kOutput, calls=%fused_computation.149 | convolution fusion | flops 2952790016 | bytes 10747904 | tf_op jit(solution)/shard_map/dot_general | solution.py:134
  228.2 5.0 fusion.98
  233.2 7.9 multiply_convert_fusion.1
  241.1 4.9 fusion.100
  246.1 5.2 convolution_add_fusion
  252.0 153.4 %all-reduce.10.cloned.1.call-done = f32[512,2048]{1,0:T(8,128)} async-done(((f32[512,2048]{1,0:T(8,128)}), f32[512,2048]{1,0:T(8,128)}) %all-reduce.10.cloned.1.call-update) | async-done | bytes 4194320 | tf_op jit(solution)/shard_map/psum | solution.py:151
  405.4 5.2 multiply_reduce_fusion
  410.6 5.3 multiply_add_fusion
  415.9 2.0 copy-done.6
  417.9 1.3 convolution_convert_fusion.8
  419.2 3.6 fusion.47
  422.8 10.6 %fusion = (f32[8,512]{1,0:T(8,128)S(1)}, f32[1024,512,8]{1,0,2:T(8,128)}) fusion(f32[1,8,512,1024]{2,3,1,0:T(8,128)} %get-tuple-element.99, f32[8,512]{1,0:T(8,128)S(1)} %log_add_fusion, bf16[512,8,64]{0,2,1:T(8,128)(2,1)S(1)} %bitcast.196, bf16[1024,64]{0,1:T(8,128)(2,1)S(1)} %all-gather), kind=kOutput, calls=%fused_computation.3 | convolution fusion | flops 549449728 | bytes 34242560 | tf_op jit(solution)/shard_map/while/body/eval_jaxpr/qhgd,khd->hgqk/dot_general | solution.py:183
  433.5 12.1 %fusion.9 = bf16[8,512,1024]{1,2,0:T(8,128)(2,1)S(1)} fusion(f32[1024,512,8]{1,0,2:T(8,128)} %get-tuple-element.101, f32[1,8,512,1024]{2,3,1,0:T(8,128)} %get-tuple-element.99, f32[8,512]{1,0:T(8,128)S(1)} %get-tuple-element.100, f32[8,512]{1,0:T(8,128)S(1)} %log_add_fusion), kind=kLoop, calls=%fused_computation.14 | loop fusion | flops 20971520 | bytes 41975808 | tf_op jit(solution)/shard_map/reshape.65
  445.6 3.3 copy-done.3
  448.9 3.3 convolution_bitcast_fusion.1
  452.4 2.4 convolution_convert_fusion.6
  454.8 4.2 reduce-scatter.10.cloned.1.call-done
  459.1 1.2 fusion.82
  460.3 1.5 convolution_convert_fusion.7
  461.8 4.8 convolution_convert_fusion.3
  466.9 5.0 convolution_bitcast_fusion
  472.1 2.9 convolution_convert_fusion.4
  475.1 8.0 convolution_convert_fusion.1
  483.1 8.0 convolution_convert_fusion.2
  491.4 7.7 convolution_convert_fusion
  499.2 8.0 convolution_convert_fusion.5
  507.2 1.3 fusion.101
  508.5 0.7 fusion.78
  509.5 2.1 add_convert_fusion
  511.6 0.6 copy-done.32
  512.2 0.6 dynamic-slice.1
  513.5 1.4 convert_element_type.213
  514.9 19.2 %reduce-scatter.16.cloned.1.call-done = bf16[256,64]{0,1:T(8,128)(2,1)} async-done(((bf16[2048,64]{0,1:T(8,128)(2,1)}), bf16[256,64]{0,1:T(8,128)(2,1)}) %reduce-scatter.16.cloned.1.call-update) | async-done | bytes 32784 | tf_op jit(solution)/shard_map/reduce_scatter | solution.py:239
  534.1 1.4 convert_element_type.211
  535.5 43.2 %reduce-scatter.20.cloned.1.call-done = bf16[512,256]{1,0:T(8,128)(2,1)} async-done(((bf16[512,2048]{1,0:T(8,128)(2,1)}), bf16[512,256]{1,0:T(8,128)(2,1)}) %reduce-scatter.20.cloned.1.call-update) | async-done | bytes 262160 | tf_op jit(solution)/shard_map/reduce_scatter | solution.py:245
  578.7 1.8 convert_element_type.215
  580.5 43.1 %reduce-scatter.14.cloned.1.call-done = bf16[256,512]{1,0:T(8,128)(2,1)} async-done(((bf16[2048,512]{1,0:T(8,128)(2,1)}), bf16[256,512]{1,0:T(8,128)(2,1)}) %reduce-scatter.14.cloned.1.call-update) | async-done | bytes 262160 | tf_op jit(solution)/shard_map/reduce_scatter | solution.py:236
  623.6 1.8 convert_element_type.209
  625.4 60.7 %reduce-scatter.24.cloned.1.call-done = bf16[256,1408]{1,0:T(8,128)(2,1)} async-done(((bf16[2048,1408]{1,0:T(8,128)(2,1)}), bf16[256,1408]{1,0:T(8,128)(2,1)}) %reduce-scatter.24.cloned.1.call-update) | async-done | bytes 720912 | tf_op jit(solution)/shard_map/reduce_scatter | solution.py:254
  686.1 2.3 convert_element_type.221
  688.4 60.5 %reduce-scatter.22.cloned.1.call-done = bf16[256,1408]{1,0:T(8,128)(2,1)} async-done(((bf16[2048,1408]{1,0:T(8,128)(2,1)}), bf16[256,1408]{1,0:T(8,128)(2,1)}) %reduce-scatter.22.cloned.1.call-update) | async-done | bytes 720912 | tf_op jit(solution)/shard_map/reduce_scatter | solution.py:251
  748.9 2.3 convert_element_type.219
  751.2 60.2 %reduce-scatter.26.cloned.1.call-done = bf16[1408,256]{1,0:T(8,128)(2,1)} async-done(((bf16[1408,2048]{1,0:T(8,128)(2,1)}), bf16[1408,256]{1,0:T(8,128)(2,1)}) %reduce-scatter.26.cloned.1.call-update) | async-done | bytes 720912 | tf_op jit(solution)/shard_map/reduce_scatter | solution.py:257
  811.4 2.3 convert_element_type.223
  813.8 156.0 %all-reduce.12.cloned.1.call-done = (bf16[512,2048]{1,0:T(8,128)(2,1)}, bf16[512,2048]{1,0:T(8,128)(2,1)}) async-done(((bf16[512,2048]{1,0:T(8,128)(2,1)}, bf16[512,2048]{1,0:T(8,128)(2,1)}), (bf16[512,2048]{1,0:T(8,128)(2,1)}, bf16[512,2048]{1,0:T(8,128)(2,1)})) %all-reduce.12.cloned.1.call-update) | async-done | bytes 4194320 | tf_op jit(solution)/shard_map/psum | solution.py:137
  969.8 2.9 fusion.28
  972.7 13.9 %all-reduce.2 = (bf16[2048]{0:T(1024)(128)(2,1)S(1)}, bf16[2048]{0:T(1024)(128)(2,1)S(1)}) all-reduce(bf16[2048]{0:T(1024)(128)(2,1)S(1)} %get-tuple-element.64, bf16[2048]{0:T(1024)(128)(2,1)S(1)} %copy-done.28), channel_id=5, replica_groups=mesh['dp'=4,'ctx'=2,'tensor'=4] {'dp','ctx'}, use_global_device_ids=true, to_apply=%region_16.17.clone | all-reduce | flops 4096 | bytes 16384
  986.6 7.8 fusion.29
  994.5 0.6 dynamic-slice_convert_fusion
  (138 shorter events, 5.6 us)
Async XLA Ops:
  7.2 45.8 %copy-start = (bf16[512,2048]{1,0:T(8,128)(2,1)S(1)}, bf16[512,2048]{1,0:T(8,128)(2,1)}, u32[]{:S(2)}) copy-start(bf16[512,2048]{1,0:T(8,128)(2,1)} %param.18) | copy-start | bytes 6291460
  7.2 10.8 %copy-start.22 = (f32[2048]{0:T(1024)S(1)}, f32[2048]{0:T(1024)}, u32[]{:S(2)}) copy-start(f32[2048]{0:T(1024)} %param.14) | copy-start | bytes 24580
  7.2 10.8 %copy-start.12 = (bf16[2048,64]{0,1:T(8,128)(2,1)S(1)}, bf16[2048,64]{0,1:T(8,128)(2,1)}, u32[]{:S(2)}) copy-start(bf16[2048,64]{0,1:T(8,128)(2,1)} %param.16) | copy-start | bytes 786436
  7.2 206.8 %all-reduce.8.cloned.1.call-start = ((), (), s32[]{:S(2)}) async-start(), calls=%async_computation.9 | async-start | bytes 8388608 | tf_op jit(solution)/shard_map/psum | solution.py:126
  7.3 12.0 %copy-start.30 = (f32[32]{0:T(128)}, f32[32]{0:T(128)S(1)}, u32[]{:S(2)}) copy-start(f32[32]{0:T(128)S(1)} %multiply_power_fusion) | copy-start | bytes 388
  12.1 13.3 %copy-start.26 = (f32[512]{0:T(512)}, f32[512]{0:T(512)S(1)}, u32[]{:S(2)}) copy-start(f32[512]{0:T(512)S(1)} %add_rsqrt_fusion.1) | copy-start | bytes 6148
  13.5 4.5 copy-start.4
  18.9 10.1 %copy-start.24 = (f32[1,512]{1,0:T(1,128)}, f32[1,512]{1,0:T(1,128)S(1)}, u32[]{:S(2)}) copy-start(f32[1,512]{1,0:T(1,128)S(1)} %fusion.84) | copy-start | bytes 6148
  25.4 3.8 copy-start.29
  37.5 8.0 copy-start.15
  45.5 7.4 copy-start.20
  53.0 3.4 copy-start.10
  56.3 161.2 %copy-start.18 = (f32[2048]{0:T(1024)S(1)}, f32[2048]{0:T(1024)}, u32[]{:S(2)}) copy-start(f32[2048]{0:T(1024)} %param.19) | copy-start | bytes 24580
  56.4 349.1 %all-reduce.10.cloned.1.call-start = ((), (), s32[]{:S(2)}) async-start(), calls=%async_computation.10 | async-start | bytes 8388608 | tf_op jit(solution)/shard_map/psum | solution.py:151
  217.5 10.6 %copy-start.2 = (f32[512,2048]{1,0:T(8,128)}, f32[512,2048]{1,0:T(8,128)S(1)}, u32[]{:S(2)}) copy-start(f32[512,2048]{1,0:T(8,128)S(1)} %get-tuple-element.71) | copy-start | bytes 12582916
  217.5 10.6 %slice-start.4 = ((s8[5767168]{0:T(1024)(128)(4,1)}), s8[4194304]{0:T(1024)(128)(4,1)S(1)}, s32[]{:S(2)}) async-start(s8[5767168]{0:T(1024)(128)(4,1)} %bitcast.210), calls=%async_computation.25 | async-start | bytes 8388608
  218.0 10.1 %copy-start.8 = (bf16[512,2048]{1,0:T(8,128)(2,1)}, bf16[512,2048]{1,0:T(8,128)(2,1)S(1)}, u32[]{:S(2)}) copy-start(bf16[512,2048]{1,0:T(8,128)(2,1)S(1)} %multiply_convert_fusion) | copy-start | bytes 6291460
  218.0 10.1 %slice-start.5 = ((s8[5767168]{0:T(1024)(128)(4,1)}), s8[1572864]{0:T(1024)(128)(4,1)S(1)}, s32[]{:S(2)}) async-start(s8[5767168]{0:T(1024)(128)(4,1)} %bitcast.210), calls=%async_computation.26 | async-start | bytes 3145728
  218.0 15.2 %slice-start.8 = ((s8[5767168]{0:T(1024)(128)(4,1)}), s8[4194304]{0:T(1024)(128)(4,1)S(1)}, s32[]{:S(2)}) async-start(s8[5767168]{0:T(1024)(128)(4,1)} %bitcast.214), calls=%async_computation.29 | async-start | bytes 8388608
  228.1 5.0 copy-start.9
  228.1 5.0 slice-start.9
  228.1 17.9 %slice-start.6 = ((s8[5767168]{0:T(1024)(128)(4,1)}), s8[4194304]{0:T(1024)(128)(4,1)S(1)}, s32[]{:S(2)}) async-start(s8[5767168]{0:T(1024)(128)(4,1)} %bitcast.212), calls=%async_computation.27 | async-start | bytes 8388608
  233.2 12.9 %slice-start.7 = ((s8[5767168]{0:T(1024)(128)(4,1)}), s8[1572864]{0:T(1024)(128)(4,1)S(1)}, s32[]{:S(2)}) async-start(s8[5767168]{0:T(1024)(128)(4,1)} %bitcast.212), calls=%async_computation.28 | async-start | bytes 3145728
  241.1 5.0 copy-start.33
  251.2 0.7 copy-start.16
  251.2 0.7 copy-start.21
  251.2 154.2 %copy-start.19 = (f32[2048]{0:T(1024)S(1)}, f32[2048]{0:T(1024)}, u32[]{:S(2)}) copy-start(f32[2048]{0:T(1024)} %param.19) | copy-start | bytes 24580
  251.3 201.1 %reduce-scatter.12.cloned.1.call-start = ((), (), s32[]{:S(2)}) async-start(), calls=%async_computation.12 | async-start | bytes 393216 | tf_op jit(solution)/shard_map/reduce_scatter | solution.py:202
  405.4 13.8 %slice-start = ((s8[16777216]{0:T(1024)(128)(4,1)}), s8[4194304]{0:T(1024)(128)(4,1)S(1)}, s32[]{:S(2)}) async-start(s8[16777216]{0:T(1024)(128)(4,1)} %bitcast.191), calls=%async_computation.21 | async-start | bytes 8388608
  405.4 13.8 %slice-start.1 = ((s8[16777216]{0:T(1024)(128)(4,1)}), s8[4194304]{0:T(1024)(128)(4,1)S(1)}, s32[]{:S(2)}) async-start(s8[16777216]{0:T(1024)(128)(4,1)} %bitcast.191), calls=%async_computation.22 | async-start | bytes 8388608
  410.6 8.6 slice-start.2
  410.6 8.6 slice-start.3
  415.9 2.0 copy-start.6
  433.4 25.7 %reduce-scatter.10.cloned.1.call-start = ((), (), s32[]{:S(2)}) async-start(), calls=%async_computation.11 | async-start | bytes 393216 | tf_op jit(solution)/shard_map/reduce_scatter | solution.py:201
  445.6 3.3 copy-start.3
  448.9 3.5 copy-start.5
  448.9 3.5 copy-start.23
  448.9 3.5 copy-start.27
  452.2 6.8 copy-start.25
  452.2 6.8 copy-start.31
  452.2 9.6 copy-start.11
  452.3 61.2 %reduce-scatter.18.cloned.1.call-start = ((), (), s32[]{:S(2)}) async-start(), calls=%async_computation.15 | async-start | bytes 294912 | tf_op jit(solution)/shard_map/reduce_scatter | solution.py:242
  454.8 79.3 %reduce-scatter.16.cloned.1.call-start = ((), (), s32[]{:S(2)}) async-start(), calls=%async_computation.14 | async-start | bytes 294912 | tf_op jit(solution)/shard_map/reduce_scatter | solution.py:239
  461.8 116.9 %reduce-scatter.20.cloned.1.call-start = ((), (), s32[]{:S(2)}) async-start(), calls=%async_computation.16 | async-start | bytes 2359296 | tf_op jit(solution)/shard_map/reduce_scatter | solution.py:245
  466.7 156.9 %reduce-scatter.14.cloned.1.call-start = ((), (), s32[]{:S(2)}) async-start(), calls=%async_computation.13 | async-start | bytes 2359296 | tf_op jit(solution)/shard_map/reduce_scatter | solution.py:236
  475.0 211.1 %reduce-scatter.24.cloned.1.call-start = ((), (), s32[]{:S(2)}) async-start(), calls=%async_computation.18 | async-start | bytes 6488064 | tf_op jit(solution)/shard_map/reduce_scatter | solution.py:254
  483.1 265.8 %reduce-scatter.22.cloned.1.call-start = ((), (), s32[]{:S(2)}) async-start(), calls=%async_computation.17 | async-start | bytes 6488064 | tf_op jit(solution)/shard_map/reduce_scatter | solution.py:251
  491.1 320.3 %reduce-scatter.26.cloned.1.call-start = ((), (), s32[]{:S(2)}) async-start(), calls=%async_computation.19 | async-start | bytes 6488064 | tf_op jit(solution)/shard_map/reduce_scatter | solution.py:257
  499.2 470.6 %all-reduce.12.cloned.1.call-start = ((), (), s32[]{:S(2)}) async-start(), calls=%async_computation.20 | async-start | bytes 8388608 | tf_op jit(solution)/shard_map/psum | solution.py:137
  499.2 8.0 copy-start.7
  507.2 1.3 copy-start.13
  508.5 1.0 copy-start.14
  508.5 1.0 copy-start.17
  511.6 0.7 copy-start.32
  688.4 284.3 %copy-start.28 = (bf16[2048]{0:T(1024)(128)(2,1)S(1)}, bf16[2048]{0:T(1024)(128)(2,1)}, u32[]{:S(2)}) copy-start(bf16[2048]{0:T(1024)(128)(2,1)} %get-tuple-element.62) | copy-start | bytes 12292
  986.6 8.5 copy-start.1
Sparse Core Ops, SparseCore 0:
  56.5 157.5 all-reduce.7
  251.4 153.9 all-reduce.9
  433.5 6.6 reduce-scatter.11
  452.4 6.6 reduce-scatter.9
  461.9 34.7 reduce-scatter.17
  500.5 33.5 reduce-scatter.15
  537.4 41.2 reduce-scatter.19
  582.3 41.2 reduce-scatter.13
  627.0 59.0 reduce-scatter.23
  689.8 59.0 reduce-scatter.21
  752.4 59.0 reduce-scatter.25
  814.4 155.3 all-reduce.11
where the time goes:
time: 1010 us; the launch traced here: 1000 us
  waiting for transfers between devices  758 us (75%)
  matrix products  129 us (13%)
  other arithmetic  65 us (6%)
  blocking collectives  19.9 us (2%)
  between operations  16.6 us (2%)
  local copies, waits for them, and re-layouts  12.1 us (1%)
    psum x1, waiting for transfers between devices, body(): lax.psum(jnp.dot(mixed_flat, out_weight, preferred_element_type=jnp.float...  157 us
    psum x1, waiting for transfers between devices, body(): lax.psum(jnp.dot(inner_act, down_weight, preferred_element_type=jnp.float...  156 us
    psum x1, waiting for transfers between devices, body(): lax.psum(jnp.dot(grad_gate_pre, gate_weight.T, preferred_element_type=jnp...  153 us
    reduce_scatter x1, waiting for transfers between devices, body(): lax.psum_scatter(grad_up.astype(jnp.bfloat16), ('dp', 'ctx'), scatter_dim...  60.7 us
    reduce_scatter x1, waiting for transfers between devices, body(): lax.psum_scatter(grad_gate.astype(jnp.bfloat16), ('dp', 'ctx'), scatter_d...  60.5 us
    reduce_scatter x1, waiting for transfers between devices, body(): lax.psum_scatter(grad_down.astype(jnp.bfloat16), ('dp', 'ctx'), scatter_d...  60.2 us
    reduce_scatter x1, waiting for transfers between devices, body(): lax.psum_scatter(grad_out_part.astype(jnp.bfloat16), ('dp', 'ctx'), scatt...  43.2 us
    reduce_scatter x1, waiting for transfers between devices, body(): lax.psum_scatter(grad_query.astype(jnp.bfloat16), ('dp', 'ctx'), scatter_...  43.1 us
  transfers between devices with their start and end apart: 12, of which 10 were waited for; matrix products, arithmetic and copies ran while one was open for 8% of the time, Pallas kernels for 0%

commit v1 on v0

--- a/solution.py
+++ b/solution.py
@@ -1,8 +1,11 @@
+import functools
 import math
 
 import jax
 import jax.numpy as jnp
 from jax import lax
+from jax.experimental import pallas as pl
+from jax.experimental.pallas import tpu as pltpu
 from jax.sharding import PartitionSpec as P
 
 HEAD_DIM = 64
@@ -17,7 +20,260 @@
     token_index = jnp.arange(segment.shape[-1], dtype=jnp.int32)
     previous = jnp.concatenate([segment[..., :1] - 1, segment[..., :-1]], axis=-1)
     starts = jnp.where(segment != previous, token_index, 0)
-    return token_index - lax.cummax(starts, axis=segment.ndim - 1)
+    earlier = token_index[None, :] <= token_index[:, None]
+    run_start = jnp.max(jnp.where(earlier, starts[..., None, :], 0), axis=-1)
+    return token_index - run_start
+
+
+MESH = pl.DeviceIdType.MESH
+CHUNK = 32
+MIB = 1 << 20
+
+
+def greet_line(line_size):
+    here = lax.axis_index("tensor")
+    barrier = pltpu.get_barrier_semaphore()
+
+    @pl.when(here > 0)
+    def _():
+        pl.semaphore_signal(barrier, inc=1, device_id={"tensor": here - 1}, device_id_type=MESH)
+
+    @pl.when(here < line_size - 1)
+    def _():
+        pl.semaphore_signal(barrier, inc=1, device_id={"tensor": here + 1}, device_id_type=MESH)
+
+    peers = jnp.where(here > 0, 1, 0) + jnp.where(here < line_size - 1, 1, 0)
+    pl.semaphore_wait(barrier, peers)
+
+
+def line_sum(line_size, own, finish, out_ref, held, acc_send, acc_recv, back_send, back_recv):
+    here = lax.axis_index("tensor")
+    last = line_size - 1
+    count = held.shape[1]
+    half = count * CHUNK
+
+    def parts(stream):
+        if stream == 0:
+            return here, here + 1, here - 1
+        return last - here, here - 1, here + 1
+
+    def acc_copy(stream, i, target):
+        return pltpu.make_async_remote_copy(
+            src_ref=held.at[stream, i],
+            dst_ref=held.at[stream, i],
+            send_sem=acc_send.at[stream, i],
+            recv_sem=acc_recv.at[stream, i],
+            device_id={"tensor": target},
+            device_id_type=MESH,
+        )
+
+    def rows_of(stream, i):
+        return pl.ds(pl.multiple_of(stream * half + i * CHUNK, CHUNK), CHUNK)
+
+    def back_copy(stream, i, target):
+        return pltpu.make_async_remote_copy(
+            src_ref=out_ref.at[rows_of(stream, i)],
+            dst_ref=out_ref.at[rows_of(stream, i)],
+            send_sem=back_send.at[stream, i],
+            recv_sem=back_recv.at[stream, i],
+            device_id={"tensor": target},
+            device_id_type=MESH,
+        )
+
+    def step(k, carry):
+        for stream in (0, 1):
+            place, after, before = parts(stream)
+            i = k - place
+
+            @pl.when((i >= 0) & (i < count) & (place == 0))
+            def _():
+                held[stream, i] = own(stream, i).astype(jnp.bfloat16)
+                acc_copy(stream, i, after).start()
+
+            @pl.when((i >= 0) & (i < count) & (place > 0) & (place < last))
+            def _():
+                acc_copy(stream, i, after).wait_recv()
+                held[stream, i] = (held[stream, i].astype(jnp.float32) + own(stream, i)).astype(
+                    jnp.bfloat16
+                )
+                acc_copy(stream, i, after).start()
+
+            @pl.when((i >= 0) & (i < count) & (place == last))
+            def _():
+                acc_copy(stream, i, before).wait_recv()
+                total = held[stream, i].astype(jnp.float32) + own(stream, i)
+                out_ref[rows_of(stream, i)] = finish(stream, i, total).astype(jnp.bfloat16)
+                back_copy(stream, i, before).start()
+
+            j = k - (2 * last - place)
+
+            @pl.when((j >= 0) & (j < count) & (place < last))
+            def _():
+                back_copy(stream, j, before).wait_recv()
+
+                @pl.when(place > 0)
+                def _():
+                    back_copy(stream, j, before).start()
+
+        return carry
+
+    lax.fori_loop(0, count + 2 * last, step, 0)
+
+    def drain(i, carry):
+        for stream in (0, 1):
+            place, after, before = parts(stream)
+
+            @pl.when(place < last)
+            def _():
+                acc_copy(stream, i, after).wait_send()
+
+            @pl.when(place > 0)
+            def _():
+                back_copy(stream, i, before).wait_send()
+
+        return carry
+
+    lax.fori_loop(0, count, drain, 0)
+
+
+def line_scratch(rows, width):
+    count = rows // 2 // CHUNK
+    return [
+        pltpu.VMEM((2, count, CHUNK, width), jnp.bfloat16),
+        pltpu.SemaphoreType.DMA((2, count)),
+        pltpu.SemaphoreType.DMA((2, count)),
+        pltpu.SemaphoreType.DMA((2, count)),
+        pltpu.SemaphoreType.DMA((2, count)),
+    ]
+
+
+def tiled_products(pairs, partial):
+    rows, width = partial.shape
+    tile_m, tile_n = min(256, rows // 2), 512
+
+    def tile(n, carry):
+        columns = pl.ds(pl.multiple_of(n * tile_n, tile_n), tile_n)
+        for m in range(rows // tile_m):
+            block = slice(m * tile_m, (m + 1) * tile_m)
+            total = None
+            for left, right, transposed in pairs:
+                if transposed:
+                    term = lax.dot_general(
+                        left[block],
+                        right[columns, :],
+                        (((1,), (1,)), ((), ())),
+                        preferred_element_type=jnp.float32,
+                    )
+                else:
+                    term = jnp.dot(
+                        left[block], right[:, columns], preferred_element_type=jnp.float32
+                    )
+                total = term if total is None else total + term
+            partial[block, columns] = total
+        return carry
+
+    lax.fori_loop(0, width // tile_n, tile, 0)
+
+
+def own_rows(partial):
+    half = partial.shape[0] // 2
+
+    def own(stream, i):
+        return partial[pl.ds(pl.multiple_of(stream * half + i * CHUNK, CHUNK), CHUNK)]
+
+    return own
+
+
+def chunk_rows(ref, stream, i):
+    half = ref.shape[0] // 2
+    return ref[pl.ds(pl.multiple_of(stream * half + i * CHUNK, CHUNK), CHUNK)]
+
+
+def kept_rows(i):
+    return pl.ds(pl.multiple_of(i * CHUNK, CHUNK), CHUNK)
+
+
+def out_kernel(n, mixed, weight, inputs, gain, normed_two, middle, partial, *scratch):
+    greet_line(n)
+    tiled_products([(mixed, weight, False)], partial)
+
+    def finish(stream, i, total):
+        value = chunk_rows(inputs, stream, i).astype(jnp.float32) + total
+        middle[kept_rows(i)] = value
+        inverse = lax.rsqrt(jnp.mean(value * value, axis=-1, keepdims=True) + epsilon)
+        return value * inverse * gain[...]
+
+    line_sum(n, own_rows(partial), finish, normed_two, *scratch)
+
+
+def down_kernel(n, inner, weight, middle, layer_out, partial, *scratch):
+    greet_line(n)
+    tiled_products([(inner, weight, False)], partial)
+
+    def finish(stream, i, total):
+        return middle[kept_rows(i)] + total
+
+    line_sum(n, own_rows(partial), finish, layer_out, *scratch)
+
+
+def back_two_kernel(
+    n, gate, up, gate_weight, up_weight, upstream, middle, gain,
+    grad_attended, grad_middle, grad_gain, partial, *scratch
+):
+    greet_line(n)
+    grad_gain[...] = jnp.zeros_like(grad_gain)
+    tiled_products([(gate, gate_weight, True), (up, up_weight, True)], partial)
+
+    def finish(stream, i, total):
+        value = middle[kept_rows(i)]
+        inverse = lax.rsqrt(jnp.mean(value * value, axis=-1, keepdims=True) + epsilon)
+        unit = value * inverse
+        grad_gain[...] += jnp.sum(total * unit, axis=0, keepdims=True)
+        scaled = total * gain[...]
+        result = chunk_rows(upstream, stream, i).astype(jnp.float32) + inverse * (
+            scaled - unit * jnp.mean(scaled * unit, axis=-1, keepdims=True)
+        )
+        grad_middle[kept_rows(i)] = result
+        return result
+
+    line_sum(n, own_rows(partial), finish, grad_attended, *scratch)
+
+
+def back_one_kernel(
+    n, query, key, value, query_weight, key_weight, value_weight, inputs, grad_middle, gain,
+    grad_inputs, grad_gain, partial, *scratch
+):
+    greet_line(n)
+    grad_gain[...] = jnp.zeros_like(grad_gain)
+    tiled_products(
+        [(query, query_weight, True), (key, key_weight, True), (value, value_weight, True)], partial
+    )
+
+    def finish(stream, i, total):
+        hidden = chunk_rows(inputs, stream, i).astype(jnp.float32)
+        inverse = lax.rsqrt(jnp.mean(hidden * hidden, axis=-1, keepdims=True) + epsilon)
+        unit = hidden * inverse
+        grad_gain[...] += jnp.sum(total * unit, axis=0, keepdims=True)
+        scaled = total * gain[...]
+        return grad_middle[kept_rows(i)] + inverse * (
+            scaled - unit * jnp.mean(scaled * unit, axis=-1, keepdims=True)
+        )
+
+    line_sum(n, own_rows(partial), finish, grad_inputs, *scratch)
+
+
+def line_call(kernel, line_size, rows, width, operands, outs, collective_id, limit):
+    vmem = pl.BlockSpec(memory_space=pltpu.VMEM)
+    return pl.pallas_call(
+        functools.partial(kernel, line_size),
+        out_shape=[jax.ShapeDtypeStruct(s, d) for s, d in outs],
+        in_specs=[vmem] * len(operands),
+        out_specs=[vmem] * len(outs),
+        scratch_shapes=[pltpu.VMEM((rows, width), jnp.float32), *line_scratch(rows, width)],
+        compiler_params=pltpu.CompilerParams(
+            collective_id=collective_id, has_side_effects=True, vmem_limit_bytes=limit * MIB
+        ),
+    )(*operands)
 
 
 def rotary_tables(positions):
@@ -123,22 +379,26 @@
         attend, (query_rows, all_keys, all_values, segment_ids, whole_segments)
     )
     mixed_flat = mixed_heads.reshape(row_count, query_heads * HEAD_DIM)
-    attended = lax.psum(
-        jnp.dot(mixed_flat, out_weight, preferred_element_type=jnp.float32), "tensor"
-    )
-    middle = hidden + attended
-    inverse_two = lax.rsqrt(jnp.mean(middle * middle, axis=-1, keepdims=True) + epsilon)
-    unit_two = middle * inverse_two
-    normed_two = (unit_two * feedforward_gain).astype(jnp.bfloat16)
+    line_size = lax.axis_size("tensor")
+    flat = (row_count, model_width)
+    kept = (row_count // 2, model_width)
+    gain_one = attention_gain.reshape(1, model_width)
+    gain_two = feedforward_gain.reshape(1, model_width)
+    flat_inputs = inputs.reshape(flat)
+    normed_two, middle = line_call(
+        out_kernel, line_size, *flat,
+        (mixed_flat, out_weight, flat_inputs, gain_two),
+        [(flat, jnp.bfloat16), (kept, jnp.float32)], 1, 28,
+    )
     gate_pre = jnp.dot(normed_two, gate_weight, preferred_element_type=jnp.float32)
     up_pre = jnp.dot(normed_two, up_weight, preferred_element_type=jnp.float32)
     sigmoid_gate = jax.nn.sigmoid(gate_pre)
     inner_act = (gate_pre * sigmoid_gate * up_pre).astype(jnp.bfloat16)
-    feed_out = lax.psum(
-        jnp.dot(inner_act, down_weight, preferred_element_type=jnp.float32).astype(jnp.bfloat16),
-        "tensor",
-    ).astype(jnp.float32)
-    layer_out = (middle + feed_out).astype(jnp.bfloat16).reshape(seq_count, span_len, model_width)
+    [layer_out] = line_call(
+        down_kernel, line_size, *flat,
+        (inner_act, down_weight, middle), [(flat, jnp.bfloat16)], 2, 28,
+    )
+    layer_out = layer_out.reshape(seq_count, span_len, model_width)
     upstream = cotangent.reshape(row_count, model_width)
     grad_down = jnp.dot(inner_act.T, upstream, preferred_element_type=jnp.float32)
     grad_inner = jnp.dot(upstream, down_weight.T, preferred_element_type=jnp.float32)
@@ -148,17 +408,11 @@
     ).astype(jnp.bfloat16)
     grad_gate = jnp.dot(normed_two.T, grad_gate_pre, preferred_element_type=jnp.float32)
     grad_up = jnp.dot(normed_two.T, grad_up_pre, preferred_element_type=jnp.float32)
-    grad_normed_two = lax.psum(
-        jnp.dot(grad_gate_pre, gate_weight.T, preferred_element_type=jnp.float32)
-        + jnp.dot(grad_up_pre, up_weight.T, preferred_element_type=jnp.float32),
-        "tensor",
-    )
-    grad_ffn_gain = jnp.sum(grad_normed_two * unit_two, axis=0)
-    scaled_two = grad_normed_two * feedforward_gain
-    grad_middle = upstream.astype(jnp.float32) + inverse_two * (
-        scaled_two - unit_two * jnp.mean(scaled_two * unit_two, axis=-1, keepdims=True)
-    )
-    grad_attended = grad_middle.astype(jnp.bfloat16)
+    grad_attended, grad_middle, grad_ffn_gain = line_call(
+        back_two_kernel, line_size, *flat,
+        (grad_gate_pre, grad_up_pre, gate_weight, up_weight, upstream, middle, gain_two),
+        [(flat, jnp.bfloat16), (kept, jnp.float32), ((1, model_width), jnp.float32)], 3, 40,
+    )
     grad_out_part = jnp.dot(mixed_flat.T, grad_attended, preferred_element_type=jnp.float32)
     grad_mixed = (
         jnp.dot(grad_attended, out_weight.T, preferred_element_type=jnp.float32)
@@ -215,24 +469,23 @@
     grad_query = jnp.dot(normed.T, grad_query_pre, preferred_element_type=jnp.float32)
     grad_key = jnp.dot(normed.T, grad_key_pre, preferred_element_type=jnp.float32)
     grad_value = jnp.dot(normed.T, grad_value_pre, preferred_element_type=jnp.float32)
-    grad_normed = lax.psum(
-        (
-            jnp.dot(grad_query_pre, query_weight.T, preferred_element_type=jnp.float32)
-            + jnp.dot(grad_key_pre, key_weight.T, preferred_element_type=jnp.float32)
-            + jnp.dot(grad_value_pre, value_weight.T, preferred_element_type=jnp.float32)
-        ).astype(jnp.bfloat16),
-        "tensor",
-    ).astype(jnp.float32)
-    grad_attn_gain = jnp.sum(grad_normed * unit_one, axis=0)
-    scaled_one = grad_normed * attention_gain
-    grad_hidden = grad_middle + inverse_one * (
-        scaled_one - unit_one * jnp.mean(scaled_one * unit_one, axis=-1, keepdims=True)
-    )
-    grad_inputs = grad_hidden.astype(jnp.bfloat16).reshape(seq_count, span_len, model_width)
+    grad_inputs, grad_attn_gain = line_call(
+        back_one_kernel, line_size, *flat,
+        (grad_query_pre, grad_key_pre, grad_value_pre, query_weight, key_weight, value_weight,
+         flat_inputs, grad_middle, gain_one),
+        [(flat, jnp.bfloat16), ((1, model_width), jnp.float32)], 4, 40,
+    )
+    grad_inputs = grad_inputs.reshape(seq_count, span_len, model_width)
+    gain_grads = jnp.concatenate([grad_attn_gain, grad_ffn_gain], axis=0)
+    place = lax.axis_index("tensor")
+    owner = (place == 0) | (place == line_size - 1)
+    gain_grads = lax.psum(jnp.where(owner, gain_grads, 0.0), ("dp", "ctx", "tensor"))
+    shards = lax.axis_size("dp") * lax.axis_size("ctx")
+    piece = model_width // shards
+    shard = lax.axis_index("dp") * lax.axis_size("ctx") + lax.axis_index("ctx")
+    gain_grads = lax.dynamic_slice_in_dim(gain_grads, shard * piece, piece, 1)
     reduced = (
-        lax.psum_scatter(
-            grad_attn_gain.astype(jnp.bfloat16), ("dp", "ctx"), scatter_dimension=0, tiled=True
-        ).astype(jnp.float32),
+        gain_grads[0],
         lax.psum_scatter(
             grad_query.astype(jnp.bfloat16), ("dp", "ctx"), scatter_dimension=0, tiled=True
         ).astype(jnp.float32),
@@ -245,9 +498,7 @@
         lax.psum_scatter(
             grad_out_part.astype(jnp.bfloat16), ("dp", "ctx"), scatter_dimension=1, tiled=True
         ).astype(jnp.float32),
-        lax.psum_scatter(
-            grad_ffn_gain.astype(jnp.bfloat16), ("dp", "ctx"), scatter_dimension=0, tiled=True
-        ).astype(jnp.float32),
+        gain_grads[1],
         lax.psum_scatter(
             grad_gate.astype(jnp.bfloat16), ("dp", "ctx"), scatter_dimension=0, tiled=True
         ).astype(jnp.float32),

time: 1010 us -> 643 us (0.64)
  waiting for transfers between devices: 758 us -> 113 us
  Pallas kernels: 0 us -> 279 us
  blocking collectives: 19.9 us -> 47.6 us
  matrix products: 129 us -> 104 us
  other arithmetic: 65 us -> 41.1 us
  local copies, waits for them, and re-layouts: 12.1 us -> 32.7 us
    psum x3 -> x0, waiting for transfers between devices: 467 us -> none  [the longest x1 157 us: body(): lax.psum(jnp.dot(mixed_flat, out_weight, preferred_element_type=jnp.float...]
    pallas_call x0 -> x4, Pallas kernels: none -> 279 us  [line_call(): pl.pallas_call(functools.partial(kernel, line_size), out_shape=[jax.Shape...]
    reduce_scatter x1, waiting for transfers between devices: 60.7 us -> 0.01 us  [body(): lax.psum_scatter(grad_up.astype(jnp.bfloat16), ('dp', 'ctx'), scatter_dim...]
    reduce_scatter x1, waiting for transfers between devices: 43.2 us -> 0.01 us  [body(): lax.psum_scatter(grad_out_part.astype(jnp.bfloat16), ('dp', 'ctx'), scatt...]
    reduce_scatter x1, waiting for transfers between devices: 43.1 us -> 0.01 us  [body(): lax.psum_scatter(grad_query.astype(jnp.bfloat16), ('dp', 'ctx'), scatter_...]
    psum x0 -> x1, blocking collectives: none -> 41.5 us  [body(): lax.psum(jnp.where(owner, gain_grads, 0.0), ('dp', 'ctx', 'tensor'))]
    dot_general x7 -> x0, matrix products: 25.4 us -> none  [the longest x1 7.95 us: body(): jnp.dot(inner_act, down_weight, preferred_element_type=jnp.float32)]
    reduce_scatter x1, waiting for transfers between devices: 19.2 us -> 0.01 us  [body(): lax.psum_scatter(grad_key.astype(jnp.bfloat16), ('dp', 'ctx'), scatter_di...]
  transfers between devices with their start and end apart: 12 -> 9, of which waited for: 10 -> 3; matrix products, arithmetic and copies ran while one was open for 8% -> 12% of each run, Pallas kernels for 0% -> 21%
where the time goes in v1:
time: 643 us; the launch traced here: 634 us
  Pallas kernels  279 us (43%)
  waiting for transfers between devices  113 us (18%)
  matrix products  104 us (16%)
  blocking collectives  47.6 us (7%)
  other arithmetic  41.1 us (6%)
  local copies, waits for them, and re-layouts  32.7 us (5%)
  between operations  15.6 us (2%)
    pallas_call x4, Pallas kernels, line_call(): pl.pallas_call(functools.partial(kernel, line_size), out_shape=[jax.Shape...  279 us
    reduce_scatter x1, waiting for transfers between devices, body(): lax.psum_scatter(grad_down.astype(jnp.bfloat16), ('dp', 'ctx'), scatter_d...  60.2 us
    reduce_scatter x1, waiting for transfers between devices, body(): lax.psum_scatter(grad_gate.astype(jnp.bfloat16), ('dp', 'ctx'), scatter_d...  46.4 us
    psum x1, blocking collectives, body(): lax.psum(jnp.where(owner, gain_grads, 0.0), ('dp', 'ctx', 'tensor'))  41.5 us
    unnamed x125, local copies, waits for them, and re-layouts  29.3 us
    convert_element_type x7, other arithmetic, body(): reduced = (gain_grads[0], lax.psum_scatter(grad_query.astype(jnp.bfloat16...  13.7 us
  transfers between devices with their start and end apart: 9, of which 3 were waited for; matrix products, arithmetic and copies ran while one was open for 12% of the time, Pallas kernels for 21%

profile of v1, /device:TPU:0, one launch (start us, length us, event | category | flops | bytes accessed | tf_op | source)
XLA Modules:
  0.0 633.6 jit_solution(8565997086571243574)
XLA Ops:
  7.3 2.1 all_gather.10
  11.0 2.2 fusion.15
  14.3 2.4 convolution_convert_fusion.8
  16.7 2.0 all-gather
  18.8 0.8 convolution_bitcast_fusion.2
  19.6 0.9 fusion.62
  20.5 1.2 fusion.50
  21.8 2.0 all_gather.11
  23.8 4.0 copy.67
  27.9 3.0 fusion.27
  31.1 1.0 fusion.25
  32.1 7.3 %fusion.76 = (f32[8,512]{1,0:T(8,128)S(1)}, f32[1,8,512,1024]{2,3,1,0:T(8,128)}) fusion(bf16[512,8,32]{0,2,1:T(8,128)(2,1)S(1)} %get-tuple-element.94, bf16[512,8,32]{0,2,1:T(8,128)(2,1)S(1)} %get-tuple-element.93, bf16[1,1024,1,64]{3,1,2,0:T(8,128)(2,1)S(1)} %all_gather.11, pred[512,1024]{0,1:T(8,128)(4,1)S(1)} %fusion.25), kind=kOutput, calls=%fused_computation.113 | convolution fusion | flops 550498304 | bytes 17973248 | tf_op jit(solution)/shard_map/while/body/eval_jaxpr/qhgd,khd->hgqk/dot_general | solution.py:362
  39.3 8.1 %fusion.4 = f32[8,512]{1,0:T(8,128)S(1)} fusion(f32[1,8,512,1024]{2,3,1,0:T(8,128)} %get-tuple-element.105, f32[8,512]{1,0:T(8,128)S(1)} %get-tuple-element.104), kind=kLoop, calls=%fused_computation.10 | loop fusion | flops 8384512 | bytes 16809984 | tf_op jit(solution)/shard_map/while/body/eval_jaxpr/reduce_sum | solution.py:368
  48.0 7.4 %fusion.30 = bf16[64,8,512]{2,0,1:T(8,128)(2,1)S(1)} fusion(f32[8,512]{1,0:T(8,128)S(1)} %fusion.4, f32[1,8,512,1024]{2,3,1,0:T(8,128)} %get-tuple-element.105, f32[8,512]{1,0:T(8,128)S(1)} %get-tuple-element.104, bf16[1024,64]{0,1:T(8,128)(2,1)S(1)} %copy-done.39), kind=kOutput, calls=%fused_computation.52 | convolution fusion | flops 549715968 | bytes 17465344 | tf_op jit(solution)/shard_map/while/body/eval_jaxpr/hgqk,khd->qhgd/dot_general | solution.py:370
  55.7 1.6 copy-done.10
  57.3 70.7 %shard_map.203 = (bf16[512,2048]{1,0:T(8,128)(2,1)S(1)}, f32[256,2048]{1,0:T(8,128)S(1)}) custom-call(bf16[512,512]{1,0:T(8,128)(2,1)S(1)} %copy.70.mixed, bf16[512,2048]{1,0:T(8,128)(2,1)S(1)} %copy-done.10, bf16[512,2048]{1,0:T(8,128)(2,1)S(1)} %bitcast.161, f32[1,2048]{1,0:T(1,128)S(1)} %bitcast.168), custom_call_target="tpu_custom_call" | custom-call | tf_op jit(solution)/shard_map/pallas_call | solution.py:267
  128.0 9.1 %fusion.78 = f32[512,1408]{1,0:T(8,128)} fusion(bf16[512,2048]{1,0:T(8,128)(2,1)S(1)} %get-tuple-element.69, bf16[2048,1408]{1,0:T(8,128)(2,1)} %up_weight.1), kind=kOutput, calls=%fused_computation.115 | convolution fusion | flops 2952790016 | bytes 10747904 | tf_op jit(solution)/shard_map/dot_general | solution.py:394
  137.2 5.0 fusion.77
  142.2 6.6 %multiply_convert_fusion = (bf16[512,1408]{1,0:T(8,128)(2,1)S(1)}, bf16[512,1408]{1,0:T(8,128)(2,1)S(1)}, bf16[512,1408]{1,0:T(8,128)(2,1)S(1)}) fusion(f32[512,1408]{1,0:T(8,128)} %fusion.77, f32[512,1408]{1,0:T(8,128)} %fusion.78, bf16[1408,2048]{1,0:T(8,128)(2,1)S(1)} %bitcast.165, bf16[1,512,2048]{2,1,0:T(8,128)(2,1)S(1)} %copy-done.14), kind=kOutput, calls=%fused_computation.34 | convolution fusion | flops 2964324352 | bytes 17956864 | tf_op jit(solution)/shard_map/dot_general | solution.py:404
  148.8 74.3 %shard_map.205 = (bf16[512,2048]{1,0:T(8,128)(2,1)S(1)}, f32[256,2048]{1,0:T(8,128)S(1)}, f32[1,2048]{1,0:T(1,128)S(1)}) custom-call(bf16[512,1408]{1,0:T(8,128)(2,1)S(1)} %get-tuple-element.89.gate, bf16[512,1408]{1,0:T(8,128)(2,1)S(1)} %get-tuple-element.88.up, bf16[2048,1408]{1,0:T(8,128)(2,1)} %gate_weight.1, bf16[2048,1408]{1,0:T(8,128)(2,1)} %up_weight.1, ...), custom_call_target="tpu_custom_call" | custom-call | tf_op jit(solution)/shard_map/pallas_call | solution.py:267
  223.2 1.3 convolution_convert_fusion.7
  224.5 0.7 copy-done.28
  225.2 0.8 copy-done.30
  226.0 8.9 %fusion.33 = f32[1,1024,1,64]{3,1,2,0:T(8,128)} fusion(bf16[512,8,64]{0,2,1:T(8,128)(2,1)S(1)} %bitcast.173, f32[1,8,512,1024]{2,3,1,0:T(8,128)} %get-tuple-element.105, f32[8,512]{1,0:T(8,128)S(1)} %copy-done.41), kind=kOutput, calls=%fused_computation.53 | convolution fusion | flops 545259520 | bytes 17580032 | tf_op jit(solution)/shard_map/while/body/eval_jaxpr/hgqk,qhgd->khd/dot_general | solution.py:434
  235.0 9.5 %fusion = (f32[8,512]{1,0:T(8,128)S(1)}, f32[1024,512,8]{1,0,2:T(8,128)S(1)}) fusion(f32[1,8,512,1024]{2,3,1,0:T(8,128)} %get-tuple-element.105, f32[8,512]{1,0:T(8,128)} %log_add_fusion, bf16[512,8,64]{0,2,1:T(8,128)(2,1)} %bitcast.174, bf16[1024,64]{0,1:T(8,128)(2,1)} %all-gather), kind=kOutput, calls=%fused_computation.3 | convolution fusion | flops 549449728 | bytes 34242560 | tf_op jit(solution)/shard_map/while/body/eval_jaxpr/qhgd,khd->hgqk/dot_general | solution.py:437
  244.6 8.0 %fusion.9 = bf16[8,512,1024]{1,2,0:T(8,128)(2,1)S(1)} fusion(f32[1024,512,8]{1,0,2:T(8,128)S(1)} %get-tuple-element.107, f32[1,8,512,1024]{2,3,1,0:T(8,128)} %get-tuple-element.105, f32[8,512]{1,0:T(8,128)S(1)} %get-tuple-element.106, f32[8,512]{1,0:T(8,128)S(1)} %copy-done.42), kind=kLoop, calls=%fused_computation.14 | loop fusion | flops 20971520 | bytes 41975808 | tf_op jit(solution)/shard_map/reshape.65
  252.6 3.3 copy-done.29
  255.9 3.1 convolution_bitcast_fusion.1
  259.1 1.0 convert_bitcast_fusion.1.value
  260.1 2.1 convolution_convert_fusion.5
  263.2 5.8 reduce-scatter.10.cloned.1.call-done
  268.9 2.2 fusion.61
  271.3 2.1 convolution_convert_fusion.6
  274.1 4.3 convolution_convert_fusion.3
  278.5 5.2 convolution_bitcast_fusion
  284.0 0.8 copy-done.31
  284.8 2.9 convolution_convert_fusion.4
  287.7 7.9 %convolution_convert_fusion.1 = bf16[2048,1408]{1,0:T(8,128)(2,1)} fusion(bf16[512,2048]{1,0:T(8,128)(2,1)} %copy-done.27, bf16[512,1408]{1,0:T(8,128)(2,1)} %copy-done.18), kind=kOutput, calls=%fused_computation.19 | convolution fusion | flops 2955673600 | bytes 9306112 | tf_op jit(solution)/shard_map/dot_general | solution.py:410
  295.7 8.0 %convolution_convert_fusion.2 = bf16[2048,1408]{1,0:T(8,128)(2,1)} fusion(bf16[512,2048]{1,0:T(8,128)(2,1)} %copy-done.27, bf16[512,1408]{1,0:T(8,128)(2,1)} %copy-done.17), kind=kOutput, calls=%fused_computation.20 | convolution fusion | flops 2955673600 | bytes 9306112 | tf_op jit(solution)/shard_map/dot_general | solution.py:409
  304.1 7.2 %convolution_convert_fusion = bf16[1408,2048]{1,0:T(8,128)(2,1)} fusion(bf16[512,1408]{1,0:T(8,128)(2,1)S(1)} %get-tuple-element.90.inner, bf16[1,512,2048]{2,1,0:T(8,128)(2,1)} %param.23), kind=kOutput, calls=%fused_computation.18 | convolution fusion | flops 2955673600 | bytes 9306112 | tf_op jit(solution)/shard_map/dot_general | solution.py:403
  311.3 0.9 copy-done.44
  312.8 1.6 copy-done.5
  314.4 2.7 copy-done.6
  317.1 1.4 copy-done.16
  318.4 70.8 %shard_map.204 = bf16[512,2048]{1,0:T(8,128)(2,1)S(1)} custom-call(bf16[512,1408]{1,0:T(8,128)(2,1)S(1)} %copy-done.16, bf16[1408,2048]{1,0:T(8,128)(2,1)S(1)} %copy-done.6, f32[256,2048]{1,0:T(8,128)S(1)} %copy-done.5), custom_call_target="tpu_custom_call" | custom-call | tf_op jit(solution)/shard_map/pallas_call | solution.py:267
  389.2 1.3 copy-done.2
  390.5 2.0 copy.77.query
  392.6 1.6 copy-done.1
  394.2 1.6 copy-done.8
  395.8 1.1 copy-done.9
  396.8 63.3 %shard_map.206 = (bf16[512,2048]{1,0:T(8,128)(2,1)S(1)}, f32[1,2048]{1,0:T(1,128)S(1)}) custom-call(bf16[512,512]{1,0:T(8,128)(2,1)S(1)} %copy-done.9, bf16[512,64]{1,0:T(8,128)(2,1)S(1)} %copy-done.22, bf16[512,64]{1,0:T(8,128)(2,1)S(1)} %copy-done.20, bf16[2048,512]{1,0:T(8,128)(2,1)S(1)} %copy-done.1, bf16[2048,64]{1,0:T(8,128)(2,1)S(1)} %copy.78.key_weight, ...), custom_call_target="tpu_custom_call" | custom-call | tf_op jit(solution)/shard_map/pallas_call | solution.py:267
  460.2 1.3 copy-done.12
  461.5 41.5 %psum.7 = f32[2,2048]{1,0:T(2,128)S(1)} all-reduce(f32[2,2048]{1,0:T(2,128)S(1)} %maximum_select_fusion), channel_id=1, replica_groups=mesh['dp'=4,'ctx'=2,'tensor'=4] {'dp','ctx','tensor'}, use_global_device_ids=true, to_apply=%region_7.8 | all-reduce | flops 4096 | bytes 32768 | tf_op jit(solution)/shard_map/psum | solution.py:482
  503.6 1.4 convert_element_type.163
  505.0 1.4 convert_element_type.161
  506.4 1.8 convert_element_type.165
  508.2 1.8 convert_element_type.159
  510.1 2.5 convert_element_type.169
  512.6 46.4 %reduce-scatter.22.cloned.1.call-done = bf16[256,1408]{1,0:T(8,128)(2,1)} async-done(((bf16[2048,1408]{1,0:T(8,128)(2,1)}), bf16[256,1408]{1,0:T(8,128)(2,1)}) %reduce-scatter.22.cloned.1.call-update) | async-done | bytes 720912 | tf_op jit(solution)/shard_map/reduce_scatter | solution.py:502
  559.0 2.3 convert_element_type.167
  561.3 60.2 %reduce-scatter.26.cloned.1.call-done = bf16[1408,256]{1,0:T(8,128)(2,1)} async-done(((bf16[1408,2048]{1,0:T(8,128)(2,1)}), bf16[1408,256]{1,0:T(8,128)(2,1)}) %reduce-scatter.26.cloned.1.call-update) | async-done | bytes 720912 | tf_op jit(solution)/shard_map/reduce_scatter | solution.py:508
  621.5 2.5 convert_element_type.171
  624.0 1.3 copy.95
  625.3 1.3 copy.96
  (151 shorter events, 7.3 us)
Async XLA Ops:
  7.2 252.0 %reduce-scatter.12.cloned.1.call-start = ((), (), s32[]{:S(2)}) async-start(), calls=%async_computation.10 | async-start | bytes 786432 | tf_op jit(solution)/shard_map/reduce_scatter | solution.py:456
  7.2 13.3 %copy-start.51 = (f32[32]{0:T(128)}, f32[32]{0:T(128)S(1)}, u32[]{:S(2)}) copy-start(f32[32]{0:T(128)S(1)} %multiply_power_fusion) | copy-start | bytes 388
  11.0 7.8 %copy-start = (bf16[1,512,2048]{2,1,0:T(8,128)(2,1)S(1)}, bf16[1,512,2048]{2,1,0:T(8,128)(2,1)}, u32[]{:S(2)}) copy-start(bf16[1,512,2048]{2,1,0:T(8,128)(2,1)} %param.12) | copy-start | bytes 6291460
  11.0 7.8 %copy-start.24 = (f32[2048]{0:T(1024)S(1)}, f32[2048]{0:T(1024)}, u32[]{:S(2)}) copy-start(f32[2048]{0:T(1024)} %param.14) | copy-start | bytes 24580
  11.0 7.8 %copy-start.43 = (bf16[2048,64]{0,1:T(8,128)(2,1)S(1)}, bf16[2048,64]{0,1:T(8,128)(2,1)}, u32[]{:S(2)}) copy-start(bf16[2048,64]{0,1:T(8,128)(2,1)} %param.16) | copy-start | bytes 786436
  13.2 6.3 copy-start.54
  19.6 8.3 %copy-start.47 = (f32[1,512]{1,0:T(1,128)}, f32[1,512]{1,0:T(1,128)S(1)}, u32[]{:S(2)}) copy-start(f32[1,512]{1,0:T(1,128)S(1)} %fusion.63) | copy-start | bytes 6148
  20.5 10.3 %copy-start.37 = (f32[512,32]{0,1:T(8,128)}, f32[512,32]{0,1:T(8,128)S(1)}, u32[]{:S(2)}) copy-start(f32[512,32]{0,1:T(8,128)S(1)} %get-tuple-element.103) | copy-start | bytes 196612
  23.8 8.2 %copy-start.32 = (bf16[1,1024,1,64]{3,1,2,0:T(8,128)(2,1)}, bf16[1,1024,1,64]{3,1,2,0:T(8,128)(2,1)S(1)}, u32[]{:S(2)}) copy-start(bf16[1,1024,1,64]{3,1,2,0:T(8,128)(2,1)S(1)} %all_gather.11) | copy-start | bytes 393220
  27.8 3.2 copy-start.49
  27.9 3.2 copy-start.50
  27.9 3.2 copy-start.53
  31.0 8.3 %copy-start.33 = (bf16[512,8,32]{0,2,1:T(8,128)(2,1)}, bf16[512,8,32]{0,2,1:T(8,128)(2,1)S(1)}, u32[]{:S(2)}) copy-start(bf16[512,8,32]{0,2,1:T(8,128)(2,1)S(1)} %get-tuple-element.93) | copy-start | bytes 786436
  31.0 8.3 %copy-start.35 = (bf16[512,8,32]{0,2,1:T(8,128)(2,1)}, bf16[512,8,32]{0,2,1:T(8,128)(2,1)S(1)}, u32[]{:S(2)}) copy-start(bf16[512,8,32]{0,2,1:T(8,128)(2,1)S(1)} %get-tuple-element.94) | copy-start | bytes 786436
  39.3 8.7 %copy-start.39 = (bf16[1024,64]{0,1:T(8,128)(2,1)S(1)}, bf16[1024,64]{0,1:T(8,128)(2,1)}, u32[]{:S(2)}) copy-start(bf16[1024,64]{0,1:T(8,128)(2,1)} %all-gather) | copy-start | bytes 393220
  48.0 7.6 %copy-start.23 = (f32[2048]{0:T(1024)S(1)}, f32[2048]{0:T(1024)}, u32[]{:S(2)}) copy-start(f32[2048]{0:T(1024)} %param.19) | copy-start | bytes 24580
  55.4 72.5 %copy-start.40 = (bf16[64,8,512]{2,0,1:T(8,128)(2,1)}, bf16[64,8,512]{2,0,1:T(8,128)(2,1)S(1)}, u32[]{:S(2)}) copy-start(bf16[64,8,512]{2,0,1:T(8,128)(2,1)S(1)} %fusion.30) | copy-start | bytes 1572868
  55.7 1.6 copy-start.10
  57.3 79.9 %slice-start.2 = ((s8[5767168]{0:T(1024)(128)(4,1)}), s8[4194304]{0:T(1024)(128)(4,1)S(1)}, s32[]{:S(2)}) async-start(s8[5767168]{0:T(1024)(128)(4,1)} %bitcast.171), calls=%async_computation.20 | async-start | bytes 8388608
  128.0 9.2 %copy-start.27 = (bf16[512,2048]{1,0:T(8,128)(2,1)}, bf16[512,2048]{1,0:T(8,128)(2,1)S(1)}, u32[]{:S(2)}) copy-start(bf16[512,2048]{1,0:T(8,128)(2,1)S(1)} %get-tuple-element.69) | copy-start | bytes 6291460
  128.0 20.9 %copy-start.4 = (f32[256,2048]{1,0:T(8,128)}, f32[256,2048]{1,0:T(8,128)S(1)}, u32[]{:S(2)}) copy-start(f32[256,2048]{1,0:T(8,128)S(1)} %get-tuple-element.70.middle) | copy-start | bytes 6291460
  128.0 9.2 %slice-start.3 = ((s8[5767168]{0:T(1024)(128)(4,1)}), s8[1572864]{0:T(1024)(128)(4,1)S(1)}, s32[]{:S(2)}) async-start(s8[5767168]{0:T(1024)(128)(4,1)} %bitcast.171), calls=%async_computation.21 | async-start | bytes 3145728
  128.0 14.2 %slice-start = ((s8[5767168]{0:T(1024)(128)(4,1)}), s8[4194304]{0:T(1024)(128)(4,1)S(1)}, s32[]{:S(2)}) async-start(s8[5767168]{0:T(1024)(128)(4,1)} %bitcast.164), calls=%async_computation.18 | async-start | bytes 8388608
  137.2 5.0 slice-start.1
  137.2 5.0 copy-start.14
  148.8 74.4 %copy-start.17 = (bf16[512,1408]{1,0:T(8,128)(2,1)}, bf16[512,1408]{1,0:T(8,128)(2,1)S(1)}, u32[]{:S(2)}) copy-start(bf16[512,1408]{1,0:T(8,128)(2,1)S(1)} %get-tuple-element.89.gate) | copy-start | bytes 4325380
  148.8 74.4 %copy-start.18 = (bf16[512,1408]{1,0:T(8,128)(2,1)}, bf16[512,1408]{1,0:T(8,128)(2,1)S(1)}, u32[]{:S(2)}) copy-start(bf16[512,1408]{1,0:T(8,128)(2,1)S(1)} %get-tuple-element.88.up) | copy-start | bytes 4325380
  148.8 155.2 %copy-start.15 = (bf16[512,1408]{1,0:T(8,128)(2,1)}, bf16[512,1408]{1,0:T(8,128)(2,1)S(1)}, u32[]{:S(2)}) copy-start(bf16[512,1408]{1,0:T(8,128)(2,1)S(1)} %get-tuple-element.90.inner) | copy-start | bytes 4325380
  148.8 74.4 %copy-start.11 = (bf16[512,2048]{1,0:T(8,128)(2,1)S(1)}, bf16[512,2048]{1,0:T(8,128)(2,1)}, u32[]{:S(2)}) copy-start(bf16[512,2048]{1,0:T(8,128)(2,1)} %weight.2) | copy-start | bytes 6291460
  223.2 1.3 copy-start.7
  223.2 1.3 copy-start.25
  223.2 2.0 copy-start.28
  223.2 2.8 copy-start.41
  235.0 33.9 %reduce-scatter.10.cloned.1.call-start = ((), (), s32[]{:S(2)}) async-start(), calls=%async_computation.9 | async-start | bytes 786432 | tf_op jit(solution)/shard_map/reduce_scatter | solution.py:455
  235.0 9.5 %copy-start.42 = (f32[8,512]{1,0:T(8,128)S(1)}, f32[8,512]{1,0:T(8,128)}, u32[]{:S(2)}) copy-start(f32[8,512]{1,0:T(8,128)} %log_add_fusion) | copy-start | bytes 49156
  244.6 11.4 %copy-start.34 = (bf16[512,8,32]{0,2,1:T(8,128)(2,1)S(1)}, bf16[512,8,32]{0,2,1:T(8,128)(2,1)}, u32[]{:S(2)}) copy-start(bf16[512,8,32]{0,2,1:T(8,128)(2,1)} %copy-done.33) | copy-start | bytes 786436
  244.6 11.4 %copy-start.36 = (bf16[512,8,32]{0,2,1:T(8,128)(2,1)S(1)}, bf16[512,8,32]{0,2,1:T(8,128)(2,1)}, u32[]{:S(2)}) copy-start(bf16[512,8,32]{0,2,1:T(8,128)(2,1)} %copy-done.35) | copy-start | bytes 786436
  252.6 3.3 copy-start.29
  259.0 9.9 %copy-start.48 = (f32[1,512]{1,0:T(1,128)S(1)}, f32[1,512]{1,0:T(1,128)}, u32[]{:S(2)}) copy-start(f32[1,512]{1,0:T(1,128)} %copy-done.47) | copy-start | bytes 6148
  259.0 9.9 %copy-start.52 = (f32[32]{0:T(128)S(1)}, f32[32]{0:T(128)}, u32[]{:S(2)}) copy-start(f32[32]{0:T(128)} %copy-done.51) | copy-start | bytes 388
  259.1 244.6 %reduce-scatter.18.cloned.1.call-start = ((), (), s32[]{:S(2)}) async-start(), calls=%async_computation.13 | async-start | bytes 294912 | tf_op jit(solution)/shard_map/reduce_scatter | solution.py:495
  262.9 242.1 %reduce-scatter.16.cloned.1.call-start = ((), (), s32[]{:S(2)}) async-start(), calls=%async_computation.12 | async-start | bytes 294912 | tf_op jit(solution)/shard_map/reduce_scatter | solution.py:492
  274.1 232.4 %reduce-scatter.20.cloned.1.call-start = ((), (), s32[]{:S(2)}) async-start(), calls=%async_computation.14 | async-start | bytes 2359296 | tf_op jit(solution)/shard_map/reduce_scatter | solution.py:498
  278.5 6.3 copy-start.55
  278.5 229.7 %reduce-scatter.14.cloned.1.call-start = ((), (), s32[]{:S(2)}) async-start(), calls=%async_computation.11 | async-start | bytes 2359296 | tf_op jit(solution)/shard_map/reduce_scatter | solution.py:489
  278.5 5.2 copy-start.38
  278.5 5.2 copy-start.46
  287.7 222.4 %reduce-scatter.24.cloned.1.call-start = ((), (), s32[]{:S(2)}) async-start(), calls=%async_computation.16 | async-start | bytes 6488064 | tf_op jit(solution)/shard_map/reduce_scatter | solution.py:505
  295.7 263.3 %reduce-scatter.22.cloned.1.call-start = ((), (), s32[]{:S(2)}) async-start(), calls=%async_computation.15 | async-start | bytes 6488064 | tf_op jit(solution)/shard_map/reduce_scatter | solution.py:502
  303.7 317.8 %reduce-scatter.26.cloned.1.call-start = ((), (), s32[]{:S(2)}) async-start(), calls=%async_computation.17 | async-start | bytes 6488064 | tf_op jit(solution)/shard_map/reduce_scatter | solution.py:508
  311.3 1.2 copy-start.45
  312.8 1.6 copy-start.5
  314.4 2.7 copy-start.6
  317.1 1.4 copy-start.16
  318.4 74.1 %copy-start.20 = (bf16[512,64]{1,0:T(8,128)(2,1)S(1)}, bf16[512,64]{1,0:T(8,128)(2,1)}, u32[]{:S(2)}) copy-start(bf16[512,64]{1,0:T(8,128)(2,1)} %copy-done.19) | copy-start | bytes 196612
  318.4 74.1 %copy-start.22 = (bf16[512,64]{1,0:T(8,128)(2,1)S(1)}, bf16[512,64]{1,0:T(8,128)(2,1)}, u32[]{:S(2)}) copy-start(bf16[512,64]{1,0:T(8,128)(2,1)} %copy-done.21) | copy-start | bytes 196612
  389.2 1.3 copy-start.2
  392.6 1.6 copy-start.1
  394.2 1.6 copy-start.8
  395.8 1.1 copy-start.9
  396.8 64.7 %copy-start.26 = (f32[1,2048]{1,0:T(1,128)S(1)}, f32[1,2048]{1,0:T(1,128)}, u32[]{:S(2)}) copy-start(f32[1,2048]{1,0:T(1,128)} %copy-done.25) | copy-start | bytes 24580
  460.2 1.3 copy-start.12
  510.1 113.9 %copy-start.3 = (bf16[512,2048]{1,0:T(8,128)(2,1)S(1)}, bf16[512,2048]{1,0:T(8,128)(2,1)}, u32[]{:S(2)}) copy-start(bf16[512,2048]{1,0:T(8,128)(2,1)} %copy-done.2) | copy-start | bytes 6291460
  621.5 3.8 copy-start.13
  (5 other events, 3.8 us)
Sparse Core Ops, SparseCore 0:
  235.1 9.6 reduce-scatter.11
  259.2 9.6 reduce-scatter.9
  272.0 34.7 reduce-scatter.17
  309.9 33.5 reduce-scatter.15
  346.7 41.2 reduce-scatter.19
  391.5 41.2 reduce-scatter.13
  436.2 59.8 reduce-scatter.23
  499.9 59.0 reduce-scatter.21
  562.4 59.0 reduce-scatter.25
